TPU v7x, 512 devices: a whole 4x8x8 slice. The times are simulated.
512 devices in a mesh: leaf: 32 (over x, y), front: 16 (over z, core).
Axes of the slice: x: 4, y: 8, z: 8, core: 2. Of those that a mesh axis runs over, the one named last changes fastest.
Arguments:
- child_pivot: float32 [32, 512, 512], P('leaf', 'front')
- child_panel: float32 [32, 2048, 512], P('leaf', 'front'), may hold values from -0.9 to 0.9
- anc_front: float32 [32, 16, 512, 512], P('leaf', 'front')
- dest_list: int32 [32, 16], replicated, may hold values from 0 to 31, as said below
- col_list: int32 [32, 16], replicated, may hold values from 0 to 3, as said below
- row_list: int32 [32, 16], replicated, may hold values from 0 to 3, as said below
Outputs:
- child_lower: float32 [32, 512, 512], P('leaf', 'front')
- child_factor: float32 [32, 2048, 512], P('leaf', 'front')
- anc_factor: float32 [32, 16, 512, 512], P('leaf', 'front')
Inputs may be any that keep to these rules, and one draw needn't show every extreme that they name: dest_list[g, j] is g with exactly one bit of its index flipped; every group that row g names is named there by exactly 4 column blocks, so row g names 4 different groups. `col_list`: column blocks of one group that name the same group in dest_list have different entries here. row_list[g, f] is 1 or more for f < 4.
All inputs are finite; a program needn't handle non-finite values.
Results may differ from a plain program's by a relative error of at most 0.0001.
Values sent between devices are 32-bit elements; how exact they have to be, the bound alone decides.
No kernel may reach another device: no remote copies, remote signals or barrier semaphores. Data moves between devices by JAX's collectives and lax.ppermute only.
A program may use at most 64 MiB of HBM per device.

v0:
```python
import jax
import jax.numpy as jnp
from jax import lax
from jax.sharding import PartitionSpec as P


def swapped(value, axis, distance):
    mask = 2**distance
    pairs = [(source, source ^ mask) for source in range(lax.axis_size(axis))]
    return lax.ppermute(value, axis, pairs)


def schur_block(left, right):
    return lax.dot_general(
        left,
        right,
        (((1,), (1,)), ((), ())),
        precision=lax.Precision.HIGHEST,
        preferred_element_type=jnp.float32,
    )


def slot_ranks(dest_list):
    count = dest_list.shape[1]
    positions = jnp.arange(count, dtype=jnp.int32)
    earlier = positions[:, None] > positions[None, :]
    same = dest_list[:, :, None] == dest_list[:, None, :]
    return jnp.sum((same & earlier[None]).astype(jnp.int32), axis=2)


def lookup_rows(table, sender_ids):
    leaf_ids = jnp.arange(table.shape[0], dtype=jnp.int32)
    hits = (sender_ids[:, None] == leaf_ids[None, :]).astype(jnp.int32)
    return jnp.sum(hits[:, :, None] * table[None], axis=1)


def pick_blocks(own_targets, own_ranks, target, slot_ids, update_blocks):
    select = ((own_targets[None, :] == target) & (own_ranks[None, :] == slot_ids[:, None])).astype(
        jnp.float32
    )
    return jnp.einsum("kj,xjy->kxy", select, update_blocks, precision=lax.Precision.HIGHEST)


def per_device(child_pivot, child_panel, anc_front, dest_list, col_list, row_list):
    front_count = lax.axis_size("front")
    front_pos = lax.axis_index("front")
    group = lax.axis_index("leaf")
    slab = child_pivot.shape[1]
    block = child_panel.shape[1]
    width = child_panel.shape[2]
    blocks_wide = width // block
    row_slots = anc_front.shape[2] // block
    pivot = lax.all_gather(child_pivot[0], "front", axis=0, tiled=True)
    lower = jnp.linalg.cholesky(pivot)
    lower_rows = lax.dynamic_slice_in_dim(lower, front_pos * slab, slab, 0)
    panel = lax.linalg.triangular_solve(
        lower, child_panel[0], left_side=False, lower=True, transpose_a=True
    )
    update = schur_block(panel, lax.all_gather(panel, "front", axis=0, tiled=True))
    ranks = slot_ranks(dest_list)
    slot_ids = jnp.arange(blocks_wide, dtype=jnp.int32)
    own_targets = lax.dynamic_index_in_dim(dest_list, group, 0, keepdims=False)
    own_ranks = lax.dynamic_index_in_dim(ranks, group, 0, keepdims=False)
    update_blocks = update.reshape(block, front_count, block)
    levels = lax.axis_size("leaf").bit_length() - 1
    arrived = []
    partners = []
    for level_bit in range(levels):
        partner = jnp.bitwise_xor(group, 1 << level_bit)
        outgoing = pick_blocks(own_targets, own_ranks, partner, slot_ids, update_blocks)
        arrived.append(swapped(outgoing, "leaf", level_bit))
        partners.append(partner)
    received = jnp.stack(arrived)
    sender_ids = jnp.stack(partners)
    src_dest = lookup_rows(dest_list, sender_ids)
    src_ranks = lookup_rows(ranks, sender_ids)
    src_cols = lookup_rows(col_list, sender_ids)
    src_rows = lookup_rows(row_list, sender_ids)
    match = (src_dest == group)[:, None, :] & (src_ranks[:, None, :] == slot_ids[None, :, None])
    live = jnp.sum(match.astype(jnp.int32), axis=2)
    column_of = jnp.sum(jnp.where(match, src_cols[:, None, :], 0), axis=2)
    row_of = lax.dynamic_index_in_dim(src_rows, front_pos, 1, keepdims=False)
    slot_rows = jnp.arange(row_slots, dtype=jnp.int32)
    slot_cols = jnp.arange(blocks_wide, dtype=jnp.int32)
    weight = (
        (live[:, :, None, None] == 1)
        & (row_of[:, None, None, None] == slot_rows[None, None, :, None])
        & (column_of[:, :, None, None] == slot_cols[None, None, None, :])
    ).astype(jnp.float32)
    incoming = jnp.einsum("gkrc,gkxy->rxcy", weight, received, precision=lax.Precision.HIGHEST)
    assembled = anc_front[0, 0] - incoming.reshape(row_slots * block, width)
    owner = front_pos < blocks_wide
    owner_pos = jnp.minimum(front_pos, blocks_wide - 1)
    top_rows = jnp.where(owner, assembled[:block], 0.0)
    contribution = lax.dynamic_update_slice_in_dim(
        jnp.zeros((width, width), jnp.float32), top_rows, owner_pos * block, 0
    )
    anc_pivot = lax.psum(contribution, "front")
    anc_lower = jnp.linalg.cholesky(anc_pivot)
    solved = lax.linalg.triangular_solve(
        anc_lower, assembled, left_side=False, lower=True, transpose_a=True
    )
    own_lower = lax.dynamic_slice_in_dim(anc_lower, owner_pos * block, block, 0)
    padded = lax.dynamic_update_slice_in_dim(jnp.zeros_like(solved), own_lower, 0, 0)
    row_ids = jnp.arange(row_slots * block, dtype=jnp.int32)
    mask = (row_ids < block)[:, None] & owner
    anc_out = jnp.where(mask, padded, solved)
    return (lower_rows[None], panel[None], anc_out[None, None])


def solution(mesh):
    in_specs = (
        P("leaf", "front", None),
        P("leaf", "front", None),
        P("leaf", "front", None, None),
        P(),
        P(),
        P(),
    )
    out_specs = (P("leaf", "front", None), P("leaf", "front", None), P("leaf", "front", None, None))
    return jax.shard_map(
        per_device, mesh=mesh, in_specs=in_specs, out_specs=out_specs, check_vma=False
    )
```

profile of v0, /device:TPU:1, one launch (start us, length us, event | category | flops | bytes accessed | tf_op | source)
XLA Modules:
  0.0 557.9 jit_solution(7262948002128751580)
XLA Ops:
  8.8 49.6 %all-gather.6.cloned.1.call-done = f32[1,512,512]{2,0,1:T(1,128)} async-done(((f32[1,32,512]{2,0,1:T(1,128)}), f32[1,512,512]{2,0,1:T(1,128)}) %all-gather.6.cloned.1.call-update) | async-done | bytes 1048592 | tf_op jit(solution)/shard_map/all_gather | solution.py:53
  61.2 11.7 %cholesky.286 = f32[128,128]{1,0:T(8,128)S(1)} custom-call(f32[128,128]{1,0:T(8,128)S(1)} %cholesky.426), custom_call_target="Cholesky" | custom-call | tf_op jit(solution)/shard_map/jit(cholesky)/cholesky | solution.py:54
  73.0 9.8 %custom-call.31 = f32[1,128,128]{1,2,0:T(8,128)S(1)} custom-call(f32[1,128,128]{2,1,0:T(8,128)S(1)} %get-tuple-element.123), custom_call_target="InvertDiagBlocksLowerTriangular" | custom-call | tf_op jit(solution)/shard_map/jit(cholesky)/cholesky | solution.py:54
  83.6 11.7 %cholesky.305 = f32[128,128]{1,0:T(8,128)S(1)} custom-call(f32[128,128]{1,0:T(8,128)S(1)} %cholesky.430), custom_call_target="Cholesky" | custom-call | tf_op jit(solution)/shard_map/jit(cholesky)/cholesky | solution.py:54
  95.5 10.0 %custom-call.32 = f32[1,128,128]{1,2,0:T(8,128)S(1)} custom-call(f32[1,128,128]{2,1,0:T(8,128)S(1)} %get-tuple-element.121), custom_call_target="InvertDiagBlocksLowerTriangular" | custom-call | tf_op jit(solution)/shard_map/jit(cholesky)/cholesky | solution.py:54
  106.6 11.7 %cholesky.326 = f32[128,128]{1,0:T(8,128)S(1)} custom-call(f32[128,128]{1,0:T(8,128)S(1)} %cholesky.435), custom_call_target="Cholesky" | custom-call | tf_op jit(solution)/shard_map/jit(cholesky)/cholesky | solution.py:54
  118.4 9.8 %custom-call.33 = f32[1,128,128]{1,2,0:T(8,128)S(1)} custom-call(f32[1,128,128]{2,1,0:T(8,128)S(1)} %get-tuple-element.119), custom_call_target="InvertDiagBlocksLowerTriangular" | custom-call | tf_op jit(solution)/shard_map/jit(cholesky)/cholesky | solution.py:54
  129.1 12.1 %cholesky.343 = f32[128,128]{1,0:T(8,128)S(1)} custom-call(f32[128,128]{1,0:T(8,128)S(1)} %convolution_subtract_fusion.11), custom_call_target="Cholesky" | custom-call | tf_op jit(solution)/shard_map/jit(cholesky)/cholesky | solution.py:54
  147.2 8.5 %while.2 = (s32[]{:T(128)}, f32[512,512]{0,1:T(8,128)S(1)}, s32[4,2]{0,1:T(2,128)S(1)}, f32[4,128,128]{2,1,0:T(8,128)S(1)}, s32[]{:T(128)}) while((s32[]{:T(128)}, f32[512,512]{0,1:T(8,128)S(1)}, s32[4,2]{0,1:T(2,128)S(1)}, f32[4,128,128]{2,1,0:T(8,128)S(1)}, s32[]{:T(128)}) %tuple.71), condition=%wide.while_cond, body=%wide.while_body.sunk | while | flops 2 | bytes 393329 | solution.py:56
  155.6 39.3 %custom-call.26 = f32[4,128,128]{1,2,0:T(8,128)S(1)} custom-call(f32[4,128,128]{2,1,0:T(8,128)S(1)} %get-tuple-element.11), custom_call_target="InvertDiagBlocksLowerTriangular" | custom-call | tf_op jit(solution)/shard_map/triangular_solve | solution.py:56
  201.5 47.6 %all-gather.4.cloned.1.call-done = f32[2048,512]{0,1:T(8,128)} async-done(((f32[128,512]{0,1:T(8,128)}), f32[2048,512]{0,1:T(8,128)}) %all-gather.4.cloned.1.call-update) | async-done | bytes 4194320 | tf_op jit(solution)/shard_map/all_gather | solution.py:59
  249.1 4.5 convolution_bitcast_fusion
  270.3 4.5 collective-permute-start.4
  274.9 9.5 %collective-permute-done.1 = f32[4,128,128]{2,0,1:T(4,128)S(1)} collective-permute-done((f32[4,128,128]{2,0,1:T(4,128)S(1)}, f32[4,128,128]{2,0,1:T(4,128)S(1)}, u32[]{:S(2)}, u32[]{:S(2)}) %collective-permute-start.1) | collective-permute-done | bytes 262176 | tf_op jit(solution)/shard_map/ppermute | solution.py:10
  290.5 113.9 %all-reduce.4.cloned.1.call-done = f32[512,512]{0,1:T(8,128)} async-done(((f32[512,512]{0,1:T(8,128)}), f32[512,512]{0,1:T(8,128)}) %all-reduce.4.cloned.1.call-update) | async-done | bytes 1048592 | tf_op jit(solution)/shard_map/psum | solution.py:98
  407.3 11.7 %cholesky.358 = f32[128,128]{1,0:T(8,128)S(1)} custom-call(f32[128,128]{1,0:T(8,128)S(1)} %cholesky.439), custom_call_target="Cholesky" | custom-call | tf_op jit(solution)/shard_map/jit(cholesky)/cholesky | solution.py:99
  419.1 9.8 %custom-call.34 = f32[1,128,128]{1,2,0:T(8,128)S(1)} custom-call(f32[1,128,128]{2,1,0:T(8,128)S(1)} %get-tuple-element.117), custom_call_target="InvertDiagBlocksLowerTriangular" | custom-call | tf_op jit(solution)/shard_map/jit(cholesky)/cholesky | solution.py:99
  431.6 11.9 %cholesky.377 = f32[128,128]{1,0:T(8,128)S(1)} custom-call(f32[128,128]{1,0:T(8,128)S(1)} %cholesky.443), custom_call_target="Cholesky" | custom-call | tf_op jit(solution)/shard_map/jit(cholesky)/cholesky | solution.py:99
  443.6 9.8 %custom-call.35 = f32[1,128,128]{1,2,0:T(8,128)S(1)} custom-call(f32[1,128,128]{2,1,0:T(8,128)S(1)} %get-tuple-element.115), custom_call_target="InvertDiagBlocksLowerTriangular" | custom-call | tf_op jit(solution)/shard_map/jit(cholesky)/cholesky | solution.py:99
  455.4 11.7 %cholesky.398 = f32[128,128]{1,0:T(8,128)S(1)} custom-call(f32[128,128]{1,0:T(8,128)S(1)} %cholesky.448), custom_call_target="Cholesky" | custom-call | tf_op jit(solution)/shard_map/jit(cholesky)/cholesky | solution.py:99
  467.3 9.8 %custom-call.36 = f32[1,128,128]{1,2,0:T(8,128)S(1)} custom-call(f32[1,128,128]{2,1,0:T(8,128)S(1)} %get-tuple-element.113), custom_call_target="InvertDiagBlocksLowerTriangular" | custom-call | tf_op jit(solution)/shard_map/jit(cholesky)/cholesky | solution.py:99
  478.8 12.0 %cholesky.415 = f32[128,128]{1,0:T(8,128)S(1)} custom-call(f32[128,128]{1,0:T(8,128)S(1)} %convolution_subtract_fusion.9), custom_call_target="Cholesky" | custom-call | tf_op jit(solution)/shard_map/jit(cholesky)/cholesky | solution.py:99
  497.3 8.6 %while.3 = (s32[]{:T(128)}, f32[512,512]{0,1:T(8,128)S(1)}, s32[4,2]{0,1:T(2,128)S(1)}, f32[4,128,128]{2,1,0:T(8,128)S(1)}, s32[]{:T(128)}) while((s32[]{:T(128)}, f32[512,512]{0,1:T(8,128)S(1)}, s32[4,2]{0,1:T(2,128)S(1)}, f32[4,128,128]{2,1,0:T(8,128)S(1)}, s32[]{:T(128)}) %tuple.83), condition=%wide.while_cond.1, body=%wide.while_body.1.sunk | while | flops 2 | bytes 393329 | solution.py:100
  505.9 39.3 %custom-call.27 = f32[4,128,128]{1,2,0:T(8,128)S(1)} custom-call(f32[4,128,128]{2,1,0:T(8,128)S(1)} %get-tuple-element.19), custom_call_target="InvertDiagBlocksLowerTriangular" | custom-call | tf_op jit(solution)/shard_map/triangular_solve | solution.py:100
  (187 shorter events, 75.6 us)
Async XLA Ops:
  7.2 51.3 %all-gather.6.cloned.1.call-start = ((), (), s32[]{:S(2)}) async-start(), calls=%async_computation.2 | async-start | bytes 1114112 | tf_op jit(solution)/shard_map/all_gather | solution.py:53
  8.8 240.3 %all-gather.4.cloned.1.call-start = ((), (), s32[]{:S(2)}) async-start(), calls=%async_computation | async-start | bytes 4456448 | tf_op jit(solution)/shard_map/all_gather | solution.py:59
  58.5 2.4 copy-start.1
  147.2 47.8 %copy-start.4 = (f32[1,128,512]{2,1,0:T(8,128)S(1)}, f32[1,128,512]{2,1,0:T(8,128)}, u32[]{:S(2)}) copy-start(f32[1,128,512]{2,1,0:T(8,128)} %param.8) | copy-start | bytes 786436
  198.1 1.8 copy-start.5
  198.1 2.0 copy-start.6
  198.1 2.0 copy-start.7
  198.1 206.3 %all-reduce.4.cloned.1.call-start = ((), (), s32[]{:S(2)}) async-start(), calls=%async_computation.1 | async-start | bytes 2097152 | tf_op jit(solution)/shard_map/psum | solution.py:98
  254.3 20.6 %collective-permute-start = (f32[4,128,128]{2,0,1:T(4,128)S(1)}, f32[4,128,128]{2,0,1:T(4,128)S(1)}, u32[]{:S(2)}, u32[]{:S(2)}) collective-permute-start(f32[4,128,128]{2,0,1:T(4,128)S(1)} %fusion.73), channel_id=1, source_target_pairs={{0,16},{16,0},{32,48},{48,32},{64,80},{80,64},{96,112},{112,96},{1... | collective-permute-start | bytes 786440 | tf_op jit(solution)/shard_map/ppermute | solution.py:10
  257.3 27.1 %collective-permute-start.1 = (f32[4,128,128]{2,0,1:T(4,128)S(1)}, f32[4,128,128]{2,0,1:T(4,128)S(1)}, u32[]{:S(2)}, u32[]{:S(2)}) collective-permute-start(f32[4,128,128]{2,0,1:T(4,128)S(1)} %fusion.76), channel_id=1, source_target_pairs={{0,32},{16,48},{32,0},{48,16},{64,96},{80,112},{96,64},{112,80},{1... | collective-permute-start | bytes 786440 | tf_op jit(solution)/shard_map/ppermute | solution.py:10
  261.9 22.6 %collective-permute-start.2 = (f32[4,128,128]{2,0,1:T(4,128)S(1)}, f32[4,128,128]{2,0,1:T(4,128)S(1)}, u32[]{:S(2)}, u32[]{:S(2)}) collective-permute-start(f32[4,128,128]{2,0,1:T(4,128)S(1)} %fusion.79), channel_id=1, source_target_pairs={{0,64},{16,80},{32,96},{48,112},{64,0},{80,16},{96,32},{112,48},{1... | collective-permute-start | bytes 786440 | tf_op jit(solution)/shard_map/ppermute | solution.py:10
  266.7 17.7 %collective-permute-start.3 = (f32[4,128,128]{2,0,1:T(4,128)S(1)}, f32[4,128,128]{2,0,1:T(4,128)S(1)}, u32[]{:S(2)}, u32[]{:S(2)}) collective-permute-start(f32[4,128,128]{2,0,1:T(4,128)S(1)} %fusion.82), channel_id=1, source_target_pairs={{0,128},{16,144},{32,160},{48,176},{64,192},{80,208},{96,224},{112... | collective-permute-start | bytes 786440 | tf_op jit(solution)/shard_map/ppermute | solution.py:10
  270.3 14.2 %collective-permute-start.4 = (f32[4,128,128]{2,0,1:T(4,128)S(1)}, f32[4,128,128]{2,0,1:T(4,128)S(1)}, u32[]{:S(2)}, u32[]{:S(2)}) collective-permute-start(f32[4,128,128]{2,0,1:T(4,128)S(1)} %fusion.85), channel_id=1, source_target_pairs={{0,256},{16,272},{32,288},{48,304},{64,320},{80,336},{96,352},{112... | collective-permute-start | bytes 786440 | tf_op jit(solution)/shard_map/ppermute | solution.py:10
  286.7 1.0 copy-start.2
  404.4 1.7 copy-start
  406.3 1.0 copy-start.3
Sparse Core Ops, SparseCore 0:
  10.7 47.7 all-gather.5
  198.2 50.7 all-gather.3
  287.9 116.4 all-reduce.3
where the time goes:
time: 567 us; the launch traced here: 558 us
  other arithmetic  242 us (43%)
  waiting for transfers between devices  221 us (39%)
  local copies, waits for them, and re-layouts  33.7 us (6%)
  matrix products  21.9 us (4%)
  between operations  20.2 us (4%)
  starting transfers between devices  18.7 us (3%)
    psum x1, waiting for transfers between devices, per_device(): anc_pivot = lax.psum(contribution, 'front')  114 us
    another operation x15, other arithmetic, per_device(): anc_lower = jnp.linalg.cholesky(anc_pivot)  79.5 us
    another operation x14, other arithmetic, per_device(): lower = jnp.linalg.cholesky(pivot)  79 us
    all_gather x1, waiting for transfers between devices, per_device(): pivot = lax.all_gather(child_pivot[0], 'front', axis=0, tiled=True)  49.6 us
    all_gather x1, waiting for transfers between devices, per_device(): lax.all_gather(panel, 'front', axis=0, tiled=True)  47.6 us
    another operation x4, other arithmetic, per_device(): lax.linalg.triangular_solve(lower, child_panel[0], left_side=False, lower...  41.3 us
    another operation x2, other arithmetic, per_device(): lax.linalg.triangular_solve(anc_lower, assembled, left_side=False, lower=...  40.5 us
    ppermute x5, starting transfers between devices, swapped(): return lax.ppermute(value, axis, pairs)  18.6 us
  transfers between devices with their start and end apart: 8, of which 4 were waited for; matrix products, arithmetic and copies ran while one was open for 1% of the time, Pallas kernels for 0%

commit v1 on v0

--- a/solution.py
+++ b/solution.py
@@ -2,6 +2,13 @@
 import jax.numpy as jnp
 from jax import lax
 from jax.sharding import PartitionSpec as P
+
+
+def exchange_gather(x, name, dim):
+    count = lax.axis_size(name)
+    blocks = jnp.stack([x for _ in range(count)])
+    blocks = lax.all_to_all(blocks, name, split_axis=0, concat_axis=0)
+    return jnp.concatenate(blocks, axis=dim)
 
 
 def swapped(value, axis, distance):
@@ -56,7 +63,7 @@
     panel = lax.linalg.triangular_solve(
         lower, child_panel[0], left_side=False, lower=True, transpose_a=True
     )
-    update = schur_block(panel, lax.all_gather(panel, "front", axis=0, tiled=True))
+    update = schur_block(panel, exchange_gather(panel, "front", 0))
     ranks = slot_ranks(dest_list)
     slot_ids = jnp.arange(blocks_wide, dtype=jnp.int32)
     own_targets = lax.dynamic_index_in_dim(dest_list, group, 0, keepdims=False)

time: 567 us -> 621 us (1.095)
  waiting for transfers between devices: 221 us -> 263 us
    all_to_all x0 -> x1, waiting for transfers between devices: none -> 91.2 us  [exchange_gather(): blocks = lax.all_to_all(blocks, name, split_axis=0, concat_axis=0)]
    all_gather x1 -> x0, waiting for transfers between devices: 47.6 us -> none  [per_device(): lax.all_gather(panel, 'front', axis=0, tiled=True)]
    another operation x40 -> x41, local copies, waits for them, and re-layouts: 16.8 us -> 19.3 us
where the time goes in v1:
time: 621 us; the launch traced here: 611 us
  waiting for transfers between devices  263 us (42%)
  other arithmetic  242 us (39%)
  local copies, waits for them, and re-layouts  35.1 us (6%)
  matrix products  26.7 us (4%)
  starting transfers between devices  23.9 us (4%)
  between operations  20.5 us (3%)
    psum x1, waiting for transfers between devices, per_device(): anc_pivot = lax.psum(contribution, 'front')  115 us
    all_to_all x1, waiting for transfers between devices, exchange_gather(): blocks = lax.all_to_all(blocks, name, split_axis=0, concat_axis=0)  91.2 us
    another operation x15, other arithmetic, per_device(): anc_lower = jnp.linalg.cholesky(anc_pivot)  79.5 us
    another operation x14, other arithmetic, per_device(): lower = jnp.linalg.cholesky(pivot)  78.9 us
    all_gather x1, waiting for transfers between devices, per_device(): pivot = lax.all_gather(child_pivot[0], 'front', axis=0, tiled=True)  49.7 us
    another operation x4, other arithmetic, per_device(): lax.linalg.triangular_solve(lower, child_panel[0], left_side=False, lower...  40.6 us
    another operation x2, other arithmetic, per_device(): lax.linalg.triangular_solve(anc_lower, assembled, left_side=False, lower=...  40.5 us
    ppermute x5, starting transfers between devices, swapped(): return lax.ppermute(value, axis, pairs)  19.1 us
  transfers between devices with their start and end apart: 8, of which 4 were waited for; matrix products, arithmetic and copies ran while one was open for 1% of the time, Pallas kernels for 0%

profile of v1, /device:TPU:1, one launch (start us, length us, event | category | flops | bytes accessed | tf_op | source)
XLA Modules:
  0.0 611.2 jit_solution(12572366619948148588)
XLA Ops:
  8.8 49.7 %all-gather.3.cloned.1.call-done = f32[1,512,512]{2,0,1:T(1,128)} async-done(((f32[1,32,512]{2,0,1:T(1,128)}), f32[1,512,512]{2,0,1:T(1,128)}) %all-gather.3.cloned.1.call-update) | async-done | bytes 1048592 | tf_op jit(solution)/shard_map/all_gather | solution.py:60
  61.2 11.7 %cholesky.286 = f32[128,128]{1,0:T(8,128)S(1)} custom-call(f32[128,128]{1,0:T(8,128)S(1)} %cholesky.426), custom_call_target="Cholesky" | custom-call | tf_op jit(solution)/shard_map/jit(cholesky)/cholesky | solution.py:61
  73.0 9.8 %custom-call.31 = f32[1,128,128]{1,2,0:T(8,128)S(1)} custom-call(f32[1,128,128]{2,1,0:T(8,128)S(1)} %get-tuple-element.123), custom_call_target="InvertDiagBlocksLowerTriangular" | custom-call | tf_op jit(solution)/shard_map/jit(cholesky)/cholesky | solution.py:61
  83.6 11.7 %cholesky.305 = f32[128,128]{1,0:T(8,128)S(1)} custom-call(f32[128,128]{1,0:T(8,128)S(1)} %cholesky.430), custom_call_target="Cholesky" | custom-call | tf_op jit(solution)/shard_map/jit(cholesky)/cholesky | solution.py:61
  95.5 10.0 %custom-call.32 = f32[1,128,128]{1,2,0:T(8,128)S(1)} custom-call(f32[1,128,128]{2,1,0:T(8,128)S(1)} %get-tuple-element.121), custom_call_target="InvertDiagBlocksLowerTriangular" | custom-call | tf_op jit(solution)/shard_map/jit(cholesky)/cholesky | solution.py:61
  106.5 11.7 %cholesky.326 = f32[128,128]{1,0:T(8,128)S(1)} custom-call(f32[128,128]{1,0:T(8,128)S(1)} %cholesky.435), custom_call_target="Cholesky" | custom-call | tf_op jit(solution)/shard_map/jit(cholesky)/cholesky | solution.py:61
  118.4 9.8 %custom-call.33 = f32[1,128,128]{1,2,0:T(8,128)S(1)} custom-call(f32[1,128,128]{2,1,0:T(8,128)S(1)} %get-tuple-element.119), custom_call_target="InvertDiagBlocksLowerTriangular" | custom-call | tf_op jit(solution)/shard_map/jit(cholesky)/cholesky | solution.py:61
  129.0 12.1 %cholesky.343 = f32[128,128]{1,0:T(8,128)S(1)} custom-call(f32[128,128]{1,0:T(8,128)S(1)} %convolution_subtract_fusion.11), custom_call_target="Cholesky" | custom-call | tf_op jit(solution)/shard_map/jit(cholesky)/cholesky | solution.py:61
  147.1 8.5 %while.2 = (s32[]{:T(128)}, f32[512,512]{0,1:T(8,128)S(1)}, s32[4,2]{0,1:T(2,128)S(1)}, f32[4,128,128]{2,1,0:T(8,128)S(1)}, s32[]{:T(128)}) while((s32[]{:T(128)}, f32[512,512]{0,1:T(8,128)S(1)}, s32[4,2]{0,1:T(2,128)S(1)}, f32[4,128,128]{2,1,0:T(8,128)S(1)}, s32[]{:T(128)}) %tuple.71), condition=%wide.while_cond, body=%wide.while_body.sunk | while | flops 2 | bytes 393329 | solution.py:63
  155.6 39.3 %custom-call.26 = f32[4,128,128]{1,2,0:T(8,128)S(1)} custom-call(f32[4,128,128]{2,1,0:T(8,128)S(1)} %get-tuple-element.11), custom_call_target="InvertDiagBlocksLowerTriangular" | custom-call | tf_op jit(solution)/shard_map/triangular_solve | solution.py:63
  200.0 4.7 all-to-all-start
  207.0 91.2 %all-to-all-done = f32[16,128,512]{2,1,0:T(8,128)} async-done(((f32[16,128,512]{2,1,0:T(8,128)}), f32[16,128,512]{2,1,0:T(8,128)}, u32[]{:S(2)}, u32[]{:S(2)}) %all-to-all-start) | async-done | bytes 4194336 | tf_op jit(solution)/shard_map/all_to_all | solution.py:10
  298.2 6.3 %fusion.29 = f32[128,16,128]{2,0,1:T(8,128)S(1)} fusion(f32[16,128,512]{2,1,0:T(8,128)} %all-to-all-done, f32[128,128]{0,1:T(8,128)S(1)} %fusion.59, f32[128,128]{0,1:T(8,128)S(1)} %fusion.60, f32[128,128]{0,1:T(8,128)S(1)} %fusion.61, f32[128,128]{0,1:T(8,128)S(1)} %bitcast.161), kind=kOutput, calls=%fused_computation.64 | convolution fusion | flops 1610809344 | bytes 5505024 | tf_op jit(solution)/shard_map/dot_general | solution.py:21
  329.2 7.3 %collective-permute-done.1 = f32[4,128,128]{2,0,1:T(4,128)S(1)} collective-permute-done((f32[4,128,128]{2,0,1:T(4,128)S(1)}, f32[4,128,128]{2,0,1:T(4,128)S(1)}, u32[]{:S(2)}, u32[]{:S(2)}) %collective-permute-start.1) | collective-permute-done | bytes 262176 | tf_op jit(solution)/shard_map/ppermute | solution.py:17
  342.6 114.9 %all-reduce.4.cloned.1.call-done = f32[512,512]{0,1:T(8,128)} async-done(((f32[512,512]{0,1:T(8,128)}), f32[512,512]{0,1:T(8,128)}) %all-reduce.4.cloned.1.call-update) | async-done | bytes 1048592 | tf_op jit(solution)/shard_map/psum | solution.py:105
  460.3 11.7 %cholesky.358 = f32[128,128]{1,0:T(8,128)S(1)} custom-call(f32[128,128]{1,0:T(8,128)S(1)} %cholesky.439), custom_call_target="Cholesky" | custom-call | tf_op jit(solution)/shard_map/jit(cholesky)/cholesky | solution.py:106
  472.2 9.8 %custom-call.34 = f32[1,128,128]{1,2,0:T(8,128)S(1)} custom-call(f32[1,128,128]{2,1,0:T(8,128)S(1)} %get-tuple-element.117), custom_call_target="InvertDiagBlocksLowerTriangular" | custom-call | tf_op jit(solution)/shard_map/jit(cholesky)/cholesky | solution.py:106
  484.6 11.9 %cholesky.377 = f32[128,128]{1,0:T(8,128)S(1)} custom-call(f32[128,128]{1,0:T(8,128)S(1)} %cholesky.443), custom_call_target="Cholesky" | custom-call | tf_op jit(solution)/shard_map/jit(cholesky)/cholesky | solution.py:106
  496.7 9.8 %custom-call.35 = f32[1,128,128]{1,2,0:T(8,128)S(1)} custom-call(f32[1,128,128]{2,1,0:T(8,128)S(1)} %get-tuple-element.115), custom_call_target="InvertDiagBlocksLowerTriangular" | custom-call | tf_op jit(solution)/shard_map/jit(cholesky)/cholesky | solution.py:106
  508.5 11.7 %cholesky.398 = f32[128,128]{1,0:T(8,128)S(1)} custom-call(f32[128,128]{1,0:T(8,128)S(1)} %cholesky.448), custom_call_target="Cholesky" | custom-call | tf_op jit(solution)/shard_map/jit(cholesky)/cholesky | solution.py:106
  520.4 9.8 %custom-call.36 = f32[1,128,128]{1,2,0:T(8,128)S(1)} custom-call(f32[1,128,128]{2,1,0:T(8,128)S(1)} %get-tuple-element.113), custom_call_target="InvertDiagBlocksLowerTriangular" | custom-call | tf_op jit(solution)/shard_map/jit(cholesky)/cholesky | solution.py:106
  531.8 12.0 %cholesky.415 = f32[128,128]{1,0:T(8,128)S(1)} custom-call(f32[128,128]{1,0:T(8,128)S(1)} %convolution_subtract_fusion.9), custom_call_target="Cholesky" | custom-call | tf_op jit(solution)/shard_map/jit(cholesky)/cholesky | solution.py:106
  550.3 8.6 %while.3 = (s32[]{:T(128)}, f32[512,512]{0,1:T(8,128)S(1)}, s32[4,2]{0,1:T(2,128)S(1)}, f32[4,128,128]{2,1,0:T(8,128)S(1)}, s32[]{:T(128)}) while((s32[]{:T(128)}, f32[512,512]{0,1:T(8,128)S(1)}, s32[4,2]{0,1:T(2,128)S(1)}, f32[4,128,128]{2,1,0:T(8,128)S(1)}, s32[]{:T(128)}) %tuple.81), condition=%wide.while_cond.1, body=%wide.while_body.1.sunk | while | flops 2 | bytes 393329 | solution.py:107
  559.0 39.3 %custom-call.27 = f32[4,128,128]{1,2,0:T(8,128)S(1)} custom-call(f32[4,128,128]{2,1,0:T(8,128)S(1)} %get-tuple-element.19), custom_call_target="InvertDiagBlocksLowerTriangular" | custom-call | tf_op jit(solution)/shard_map/triangular_solve | solution.py:107
  (189 shorter events, 84.2 us)
Async XLA Ops:
  7.2 51.3 %all-gather.3.cloned.1.call-start = ((), (), s32[]{:S(2)}) async-start(), calls=%async_computation.2 | async-start | bytes 1114112 | tf_op jit(solution)/shard_map/all_gather | solution.py:60
  58.5 2.4 copy-start.1
  147.1 47.8 %copy-start.5 = (f32[1,128,512]{2,1,0:T(8,128)S(1)}, f32[1,128,512]{2,1,0:T(8,128)}, u32[]{:S(2)}) copy-start(f32[1,128,512]{2,1,0:T(8,128)} %param.8) | copy-start | bytes 786436
  200.0 4.8 copy-start.4
  200.0 98.2 %all-to-all-start = ((f32[16,128,512]{2,1,0:T(8,128)}), f32[16,128,512]{2,1,0:T(8,128)}, u32[]{:S(2)}, u32[]{:S(2)}) async-start(f32[16,128,512]{2,1,0:T(8,128)} %stack.26), calls=%async_computation | async-start | bytes 8388608 | tf_op jit(solution)/shard_map/all_to_all | solution.py:10
  204.7 0.7 copy-start.6
  204.7 0.9 copy-start.7
  204.7 0.9 copy-start.8
  204.7 252.7 %all-reduce.4.cloned.1.call-start = ((), (), s32[]{:S(2)}) async-start(), calls=%async_computation.1 | async-start | bytes 2097152 | tf_op jit(solution)/shard_map/psum | solution.py:105
  305.6 23.5 %collective-permute-start = (f32[4,128,128]{2,0,1:T(4,128)S(1)}, f32[4,128,128]{2,0,1:T(4,128)S(1)}, u32[]{:S(2)}, u32[]{:S(2)}) collective-permute-start(f32[4,128,128]{2,0,1:T(4,128)S(1)} %fusion.14), channel_id=1, source_target_pairs={{0,16},{16,0},{32,48},{48,32},{64,80},{80,64},{96,112},{112,96},{1... | collective-permute-start | bytes 786440 | tf_op jit(solution)/shard_map/ppermute | solution.py:17
  309.8 26.7 %collective-permute-start.1 = (f32[4,128,128]{2,0,1:T(4,128)S(1)}, f32[4,128,128]{2,0,1:T(4,128)S(1)}, u32[]{:S(2)}, u32[]{:S(2)}) collective-permute-start(f32[4,128,128]{2,0,1:T(4,128)S(1)} %fusion.12), channel_id=1, source_target_pairs={{0,32},{16,48},{32,0},{48,16},{64,96},{80,112},{96,64},{112,80},{1... | collective-permute-start | bytes 786440 | tf_op jit(solution)/shard_map/ppermute | solution.py:17
  314.9 21.6 %collective-permute-start.2 = (f32[4,128,128]{2,0,1:T(4,128)S(1)}, f32[4,128,128]{2,0,1:T(4,128)S(1)}, u32[]{:S(2)}, u32[]{:S(2)}) collective-permute-start(f32[4,128,128]{2,0,1:T(4,128)S(1)} %fusion.10), channel_id=1, source_target_pairs={{0,64},{16,80},{32,96},{48,112},{64,0},{80,16},{96,32},{112,48},{1... | collective-permute-start | bytes 786440 | tf_op jit(solution)/shard_map/ppermute | solution.py:17
  320.4 16.1 %collective-permute-start.3 = (f32[4,128,128]{2,0,1:T(4,128)S(1)}, f32[4,128,128]{2,0,1:T(4,128)S(1)}, u32[]{:S(2)}, u32[]{:S(2)}) collective-permute-start(f32[4,128,128]{2,0,1:T(4,128)S(1)} %fusion.8), channel_id=1, source_target_pairs={{0,128},{16,144},{32,160},{48,176},{64,192},{80,208},{96,224},{112... | collective-permute-start | bytes 786440 | tf_op jit(solution)/shard_map/ppermute | solution.py:17
  324.6 12.0 %collective-permute-start.4 = (f32[4,128,128]{2,0,1:T(4,128)S(1)}, f32[4,128,128]{2,0,1:T(4,128)S(1)}, u32[]{:S(2)}, u32[]{:S(2)}) collective-permute-start(f32[4,128,128]{2,0,1:T(4,128)S(1)} %fusion.6), channel_id=1, source_target_pairs={{0,256},{16,272},{32,288},{48,304},{64,320},{80,336},{96,352},{112... | collective-permute-start | bytes 786440 | tf_op jit(solution)/shard_map/ppermute | solution.py:17
  338.8 1.0 copy-start.2
  457.4 1.7 copy-start
  459.3 1.0 copy-start.3
Sparse Core Ops, SparseCore 0:
  10.7 47.7 all-gather.2
  340.0 117.4 all-reduce.3
